TPU v7x, 32 devices: a whole 2x2x4 slice. The times are simulated.
32 devices in a mesh: cls: 8 (over z, x), img: 4 (over y, core).
Axes of the slice: x: 2, y: 2, z: 4, core: 2. Of those that a mesh axis runs over, the one named last changes fastest.
Arguments:
- images: bfloat16 [512, 9216], P(('cls', 'img')), may hold values from -9 to 9
- ctf: bfloat16 [512, 4608], P(('cls', 'img')), may hold values from -1 to 1
- classes: int32 [512, 4], P(('cls', 'img')), may hold values from 0 to 55, as said below
- class_place: int32 [56], replicated, may hold values from 0 to 55, as said below
- references: bfloat16 [56, 9216], P('cls'), may hold values from -3 to 3
- sigma2: float32 [64], replicated, may hold values from 0.05 to 4, as said below
Outputs:
- new_references: float32 [56, 9216], P('cls', 'img')
Inputs may be any that keep to these rules, and one draw needn't show every extreme that they name: Each particle names 4 different classes whose table rows class_place[k] lie in 4 different groups of 7 consecutive table rows. Among the 16 particles of one device (aligned blocks of 16 rows) at most 8 list entries fall in one group, and in every block some group receives exactly 8. A permutation: class k is held in table row class_place[k]. `sigma2`: positive noise powers.
All inputs are finite; a program needn't handle non-finite values.
Results may differ from a plain program's by a relative error of at most 0.0018.
Values may be sent and summed in bfloat16 or wider, within the bound.
A program may use at most 128 MiB of HBM per device.

v0:
```python
import functools

import jax
import jax.numpy as jnp
from jax import lax
from jax.experimental import pallas as pl
from jax.experimental.pallas import tpu as pltpu
from jax.sharding import PartitionSpec as P

MESH = pl.DeviceIdType.MESH
VMEM = pltpu.VMEM
F32 = jnp.float32
BF16 = jnp.bfloat16
LANES = 128


def vmem_specs(count):
    return [pl.BlockSpec(memory_space=pltpu.VMEM)] * count


def greet(groups):
    barrier = pltpu.get_barrier_semaphore()
    total = 0
    for axis, size in groups:
        me = lax.axis_index(axis)
        for step in range(1, size):
            peer = lax.rem(me + step, size)
            pl.semaphore_signal(barrier, inc=1, device_id={axis: peer}, device_id_type=MESH)
            total += 1
    pl.semaphore_wait(barrier, total)


def spread_kernel(owners, fellows, w_ref, r_ref, t_ref, wall, rall, tall, own_sem, ws, wr, rs, rr, ts, tr):
    my_owner = lax.axis_index("cls")
    my_fellow = lax.axis_index("img")
    greet((("cls", owners), ("img", fellows)))
    copies = []
    for step in range(1, owners):
        peer = lax.rem(my_owner + step, owners)
        copies.append(
            pltpu.make_async_remote_copy(
                src_ref=r_ref,
                dst_ref=rall.at[my_owner],
                send_sem=rs.at[step],
                recv_sem=rr.at[step],
                device_id={"cls": peer},
                device_id_type=MESH,
            )
        )
    for step in range(1, fellows):
        peer = lax.rem(my_fellow + step, fellows)
        copies.append(
            pltpu.make_async_remote_copy(
                src_ref=t_ref,
                dst_ref=tall.at[my_fellow],
                send_sem=ts.at[step],
                recv_sem=tr.at[step],
                device_id={"img": peer},
                device_id_type=MESH,
            )
        )
        copies.append(
            pltpu.make_async_remote_copy(
                src_ref=w_ref.at[peer],
                dst_ref=wall.at[my_fellow],
                send_sem=ws.at[step],
                recv_sem=wr.at[step],
                device_id={"img": peer},
                device_id_type=MESH,
            )
        )
    for copy in copies:
        copy.start()
    own = [
        pltpu.make_async_copy(w_ref.at[my_fellow], wall.at[my_fellow], own_sem.at[0]),
        pltpu.make_async_copy(r_ref, rall.at[my_owner], own_sem.at[1]),
        pltpu.make_async_copy(t_ref, tall.at[my_fellow], own_sem.at[2]),
    ]
    for copy in own:
        copy.start()
    for copy in own:
        copy.wait()
    for copy in copies:
        copy.wait()


def exchange_kernel(axis, size, x_ref, out_ref, own_sem, send, recv, *, split):
    me = lax.axis_index(axis)
    greet(((axis, size),))
    copies = []
    for step in range(1, size):
        peer = lax.rem(me + step, size)
        copies.append(
            pltpu.make_async_remote_copy(
                src_ref=x_ref.at[peer] if split else x_ref,
                dst_ref=out_ref.at[me],
                send_sem=send.at[step],
                recv_sem=recv.at[step],
                device_id={axis: peer},
                device_id_type=MESH,
            )
        )
    for copy in copies:
        copy.start()
    own = pltpu.make_async_copy(x_ref.at[me] if split else x_ref, out_ref.at[me], own_sem.at[0])
    own.start()
    own.wait()
    for copy in copies:
        copy.wait()


def exchange(x, axis, size, split, collective_id):
    block = x.shape[1:] if split else x.shape
    return pl.pallas_call(
        functools.partial(exchange_kernel, axis, size, split=split),
        out_shape=jax.ShapeDtypeStruct((size,) + block, x.dtype),
        in_specs=vmem_specs(1),
        out_specs=pl.BlockSpec(memory_space=pltpu.VMEM),
        scratch_shapes=[
            pltpu.SemaphoreType.DMA((1,)),
            pltpu.SemaphoreType.DMA((size,)),
            pltpu.SemaphoreType.DMA((size,)),
        ],
        compiler_params=pltpu.CompilerParams(collective_id=collective_id, has_side_effects=True),
    )(x)


def lane_of(shape):
    return lax.broadcasted_iota(jnp.int32, shape, len(shape) - 1)


def roll(x, shift):
    return pltpu.roll(x, shift % LANES, x.ndim - 1)


def score_kernel(dims, rows_ref, wall, rall, logits_ref, weights_ref, table, low, high):
    fellows, particles, owners, slots, top, angles, half = dims
    width = 2 * half
    per_pack = LANES // width
    per_den = LANES // half
    tall_rows = table.shape[1]
    num_packs = particles // per_pack
    lane = lane_of((angles, LANES))
    zero_tail = jnp.zeros((LANES - angles, LANES), F32)

    def place(fellow, carry):
        for i in range(particles):
            num = wall[fellow, i // per_pack].astype(F32)
            den = wall[fellow, num_packs + i // per_den].astype(F32)
            num = roll(num, -width * (i % per_pack))
            den = roll(den, width - half * (i % per_den))
            joined = jnp.where(lane < width, num, jnp.where(lane < width + half, den, 0.0))
            weights_ref[fellow * particles + i] = jnp.concatenate([joined, zero_tail], axis=0).astype(BF16)
        return carry

    lax.fori_loop(0, fellows, place, 0)

    def tabulate(owner, carry):
        for t in range(slots):
            ref = roll(rall[owner, t // per_pack].astype(F32), -width * (t % per_pack))
            square = ref * ref
            power = (square + roll(square, -half)).astype(BF16).astype(F32) * -0.5
            power = roll(power, width)
            joined = jnp.where(lane < width, ref, jnp.where(lane < width + half, power, 0.0))
            table[owner * slots + t] = jnp.concatenate(
                [joined, jnp.zeros((tall_rows - angles, LANES), F32)], axis=0
            ).astype(BF16)
        return carry

    lax.fori_loop(0, owners, tabulate, 0)
    cut = (angles // 16) * 8 + (8 if (angles // 8) % 2 else 0)
    tiles = angles // 8

    def pair(m, carry):
        lows = []
        highs = []
        for k in range(2):
            i = 2 * m + k
            refs = jnp.concatenate([table[rows_ref[i, j]] for j in range(top)], axis=0)
            grid = lax.dot_general(
                refs, weights_ref[i], (((1,), (1,)), ((), ())), preferred_element_type=F32
            )
            for j in range(top):
                base = j * tall_rows
                lo = grid[base : base + 8]
                for tile in range(1, cut // 8):
                    lo = lo + roll(grid[base + 8 * tile : base + 8 * tile + 8], 8 * tile)
                hi = grid[base + cut : base + cut + 8]
                for tile in range(cut // 8 + 1, tiles):
                    hi = hi + roll(grid[base + 8 * tile : base + 8 * tile + 8], 8 * tile - cut)
                lo = pltpu.roll(lo, 0, 1, stride=1, stride_axis=0)
                hi = pltpu.roll(hi, 0, 1, stride=1, stride_axis=0)
                lows.append(jnp.sum(lo, axis=0, keepdims=True))
                highs.append(jnp.sum(hi, axis=0, keepdims=True))
        low[m] = jnp.concatenate(lows, axis=0)
        high[m] = jnp.concatenate(highs, axis=0)
        return carry

    lax.fori_loop(0, low.shape[0], pair, 0)
    lo = low[...].reshape(-1, LANES)
    hi = high[...].reshape(-1, LANES)
    spot = lane_of(lo.shape)
    total = roll(lo, 1) + jnp.where(spot < cut, roll(lo, 1 - angles), 0.0)
    back = angles - 1 - cut
    total = total + roll(hi, -back) + jnp.where(spot >= cut + 1, roll(hi, cut + 1), 0.0)
    logits_ref[...] = jnp.where(spot < angles, total, 0.0)


def group_of(x, top, combine):
    row = lax.broadcasted_iota(jnp.int32, x.shape, 0)
    count = x.shape[0]
    step = 1
    while step < top:
        swapped = jnp.where(
            (row // step) % 2 == 0, pltpu.roll(x, count - step, 0), pltpu.roll(x, step, 0)
        )
        x = combine(x, swapped)
        step *= 2
    return x


def total_kernel(dims, rows_ref, parts, weights_ref, out_ref, acc, ext_lo, ext_hi):
    fellows, particles, owners, slots, top, angles, half = dims
    width = 2 * half
    per_pack = LANES // width
    per_den = LANES // half
    num_packs = slots // per_pack
    cut = (angles // 16) * 8 + (8 if (angles // 8) % 2 else 0)
    tiles = angles // 8
    tall_rows = -(-angles // 16) * 16
    logits = parts[0]
    for fellow in range(1, fellows):
        logits = logits + parts[fellow]
    spot = lane_of(logits.shape)
    inside = spot < angles
    highest = jnp.max(jnp.where(inside, logits, -jnp.inf), axis=1, keepdims=True)
    highest = group_of(jnp.broadcast_to(highest, logits.shape), top, jnp.maximum)
    exponent = jnp.where(inside, jnp.exp(logits - highest), 0.0)
    summed = jnp.sum(exponent, axis=1, keepdims=True)
    summed = group_of(jnp.broadcast_to(summed, logits.shape), top, jnp.add)
    post = (exponent / summed).astype(BF16).astype(F32)
    lo = jnp.where(inside, post, roll(post, LANES - angles))
    hi = jnp.where((spot >= cut) & inside, roll(post, cut), roll(post, cut - angles))
    ext_lo[...] = lo.reshape(ext_lo.shape)
    ext_hi[...] = hi.reshape(ext_hi.shape)
    acc[...] = jnp.zeros_like(acc)

    def pair(m, carry):
        lo_rows = ext_lo[m]
        hi_rows = ext_hi[m]
        for k in range(2):
            i = 2 * m + k
            turned = []
            for j in range(top):
                e = k * top + j
                first = pltpu.roll(
                    jnp.broadcast_to(lo_rows[e : e + 1], (8, LANES)), 0, 1, stride=1, stride_axis=0
                )
                second = pltpu.roll(
                    jnp.broadcast_to(hi_rows[e : e + 1], (8, LANES)), 0, 1, stride=1, stride_axis=0
                )
                for tile in range(tiles):
                    if 8 * tile < cut:
                        turned.append(roll(first, 8 * tile) if tile else first)
                    else:
                        shift = 8 * tile - cut
                        turned.append(roll(second, shift) if shift else second)
                for tile in range(tiles, tall_rows // 8):
                    turned.append(second)
            circle = jnp.concatenate(turned, axis=0).astype(BF16)
            grid = jnp.dot(circle, weights_ref[i], preferred_element_type=F32)
            for j in range(top):
                row = rows_ref[i, j]
                acc[row] = acc[row] + grid[j * tall_rows : j * tall_rows + angles]
        return carry

    lax.fori_loop(0, ext_lo.shape[0], pair, 0)
    lane = lane_of((angles, LANES))

    def pack(owner, carry):
        nums = [None] * num_packs
        dens = [None] * (slots // per_den)
        for t in range(slots):
            value = acc[owner * slots + t]
            g, u = t % per_pack, t // per_pack
            num = roll(value, width * g)
            nums[u] = num if g == 0 else jnp.where(lane >= width * g, num, nums[u])
            h, v = t % per_den, t // per_den
            den = roll(value, half * h - width)
            dens[v] = den if h == 0 else jnp.where(lane >= half * h, den, dens[v])
        for u, value in enumerate(nums + dens):
            out_ref[owner, u] = value.astype(BF16)
        return carry

    lax.fori_loop(0, owners, pack, 0)


def gather_kernel(axis, size, x_ref, out_ref, landed, send, recv):
    me = lax.axis_index(axis)
    greet(((axis, size),))
    copies = []
    for step in range(1, size):
        peer = lax.rem(me + step, size)
        copies.append(
            pltpu.make_async_remote_copy(
                src_ref=x_ref.at[peer],
                dst_ref=landed.at[step - 1],
                send_sem=send.at[step],
                recv_sem=recv.at[step],
                device_id={axis: peer},
                device_id_type=MESH,
            )
        )
    for copy in copies:
        copy.start()
    total = x_ref[me].astype(F32)
    for step in range(1, size):
        copies[step - 1].wait_recv()
        total = total + landed[step - 1].astype(F32)
    out_ref[...] = total
    for copy in copies:
        copy.wait_send()


def on_device(images, ctf, classes, class_place, references, sigma2):
    shells = sigma2.shape[0]
    angles = ctf.shape[1] // shells
    particles = images.shape[0]
    per_owner = references.shape[0]
    top = classes.shape[1]
    owners = lax.axis_size("cls")
    fellows = lax.axis_size("img")
    my_fellow = lax.axis_index("img")
    half = shells // fellows
    width = 2 * half
    per_pack = LANES // width
    per_den = LANES // half
    slots = -(-per_owner // per_den) * per_den
    dims = (fellows, particles, owners, slots, top, angles, half)

    scaling = ctf.astype(F32).reshape(particles, shells, angles) * (1.0 / sigma2)[None, :, None]
    weighted = (
        images.astype(F32).reshape(particles, shells, 2, angles) * scaling[:, :, None, :]
    ).astype(BF16)
    ctf_power = (ctf.astype(F32).reshape(particles, shells, angles) * scaling).astype(BF16)
    num = weighted.reshape(particles // per_pack, per_pack, fellows, half, 2, angles)
    num = num.transpose(2, 0, 5, 1, 4, 3).reshape(fellows, -1, angles, LANES)
    den = ctf_power.reshape(particles // per_den, per_den, fellows, half, angles)
    den = den.transpose(2, 0, 4, 1, 3).reshape(fellows, -1, angles, LANES)
    send = jnp.concatenate([num, den], axis=1)
    mine = lax.dynamic_slice_in_dim(references, my_fellow * (width * angles), width * angles, 1)
    mine = jnp.pad(mine, ((0, slots - per_owner), (0, 0)))
    mine = mine.reshape(slots // per_pack, per_pack, half, 2, angles)[..., ::-1]
    mine = mine.transpose(0, 4, 1, 3, 2).reshape(-1, angles, LANES)

    lookup = classes[:, :, None] == jnp.arange(class_place.shape[0], dtype=jnp.int32)[None, None, :]
    table_rows = jnp.sum(jnp.where(lookup, class_place[None, None, :], 0), axis=2)
    rows = (table_rows // per_owner) * slots + table_rows % per_owner
    rows = jnp.pad(rows, ((0, 0), (0, LANES - top)))

    packs = send.shape[1]
    wall, rall, tall = pl.pallas_call(
        functools.partial(spread_kernel, owners, fellows),
        out_shape=(
            jax.ShapeDtypeStruct((fellows, packs, angles, LANES), BF16),
            jax.ShapeDtypeStruct((owners,) + mine.shape, BF16),
            jax.ShapeDtypeStruct((fellows, particles, LANES), jnp.int32),
        ),
        in_specs=vmem_specs(3),
        out_specs=tuple(vmem_specs(3)),
        scratch_shapes=[
            pltpu.SemaphoreType.DMA((3,)),
            pltpu.SemaphoreType.DMA((fellows,)),
            pltpu.SemaphoreType.DMA((fellows,)),
            pltpu.SemaphoreType.DMA((owners,)),
            pltpu.SemaphoreType.DMA((owners,)),
            pltpu.SemaphoreType.DMA((fellows,)),
            pltpu.SemaphoreType.DMA((fellows,)),
        ],
        compiler_params=pltpu.CompilerParams(collective_id=0, has_side_effects=True),
    )(send, mine, rows)
    everyone = fellows * particles
    row_list = tall[:, :, :top].reshape(everyone, top)
    tall_rows = -(-angles // 16) * 16
    pairs = everyone // 2
    smem = pl.BlockSpec(memory_space=pltpu.SMEM)
    logits, weights = pl.pallas_call(
        functools.partial(score_kernel, dims),
        out_shape=(
            jax.ShapeDtypeStruct((everyone * top, LANES), F32),
            jax.ShapeDtypeStruct((everyone, LANES, LANES), BF16),
        ),
        in_specs=[smem] + vmem_specs(2),
        out_specs=tuple(vmem_specs(2)),
        scratch_shapes=[
            VMEM((owners * slots, tall_rows, LANES), BF16),
            VMEM((pairs, 2 * top, LANES), F32),
            VMEM((pairs, 2 * top, LANES), F32),
        ],
    )(row_list, wall, rall)
    parts = exchange(logits, "img", fellows, False, 1)
    sums = pl.pallas_call(
        functools.partial(total_kernel, dims),
        out_shape=jax.ShapeDtypeStruct(
            (owners, slots // per_pack + slots // per_den, angles, LANES), BF16
        ),
        in_specs=[smem] + vmem_specs(2),
        out_specs=pl.BlockSpec(memory_space=pltpu.VMEM),
        scratch_shapes=[
            VMEM((owners * slots, angles, LANES), F32),
            VMEM((pairs, 2 * top, LANES), F32),
            VMEM((pairs, 2 * top, LANES), F32),
        ],
    )(row_list, parts, weights)
    share = pl.pallas_call(
        functools.partial(gather_kernel, "cls", owners),
        out_shape=jax.ShapeDtypeStruct(sums.shape[1:], F32),
        in_specs=vmem_specs(1),
        out_specs=pl.BlockSpec(memory_space=pltpu.VMEM),
        scratch_shapes=[
            VMEM((owners - 1,) + sums.shape[1:], BF16),
            pltpu.SemaphoreType.DMA((owners,)),
            pltpu.SemaphoreType.DMA((owners,)),
        ],
        compiler_params=pltpu.CompilerParams(collective_id=2, has_side_effects=True),
    )(sums)
    num_packs = slots // per_pack
    num = share[:num_packs].reshape(num_packs, angles, per_pack, 2, half)
    num = num.transpose(0, 2, 4, 3, 1).reshape(slots, half, 2, angles)[:per_owner]
    den = share[num_packs:].reshape(-1, angles, per_den, half)
    den = den.transpose(0, 2, 3, 1).reshape(slots, half, 1, angles)[:per_owner]
    return (num / (den + 1.0)).reshape(per_owner, -1)


def solution(mesh):
    in_specs = (
        P(("cls", "img"), None),
        P(("cls", "img"), None),
        P(("cls", "img"), None),
        P(),
        P("cls", None),
        P(),
    )
    out_specs = P("cls", "img")
    return jax.shard_map(
        on_device, mesh=mesh, in_specs=in_specs, out_specs=out_specs, check_vma=False
    )
```

profile of v0, /device:TPU:0, one launch (start us, length us, event | category | flops | bytes accessed | tf_op | source)
XLA Modules:
  0.0 85.1 jit_solution(6170823469432638565)
XLA Ops:
  0.0 0.7 broadcast_divide_fusion
  0.8 0.9 %select_reduce_fusion = s32[16,4]{0,1:T(4,128)S(1)} fusion(s32[56]{0:T(128)} %param.9, s32[16,4]{0,1:T(4,128)} %param.8), kind=kLoop, calls=%fused_computation.9 | loop fusion | flops 10688 | bytes 736 | tf_op jit(solution)/shard_map/reduce_sum | solution.py:357
  1.8 0.6 pad.9.t_ref
  2.5 0.2 reshape.72
  2.6 0.1 rev.3
  2.7 0.7 copy.47.r_ref
  3.5 1.4 %reshape.70 = f32[2,8,4,16,72]{4,3,2,1,0:T(8,128)S(1)} reshape(bf16[16,4608]{1,0:T(8,128)(2,1)} %param.7) | data formatting | bytes 442368 | tf_op jit(solution)/shard_map/reshape | solution.py:341
  4.9 0.1 fusion.1
  5.0 0.1 copy.42
  5.2 0.5 reshape.68
  5.7 2.1 %reshape.80 = f32[4,4,4,16,2,72]{5,4,3,2,1,0:T(2,128)S(1)} reshape(bf16[16,9216]{1,0:T(8,128)(2,1)S(1)} %copy-done.2) | data formatting | bytes 884736 | tf_op jit(solution)/shard_map/reshape | solution.py:343
  7.8 0.2 fusion
  8.1 0.2 copy.41
  8.3 0.8 pad_maximum_fusion.w_ref
  9.1 14.2 %shard_map.64 = (bf16[4,6,72,128]{3,2,1,0:T(8,128)(2,1)}, bf16[8,2,72,128]{3,2,1,0:T(8,128)(2,1)}, s32[4,16,128]{2,1,0:T(8,128)}) custom-call(bf16[4,6,72,128]{3,2,1,0:T(8,128)(2,1)} %pad_maximum_fusion.w_ref, bf16[2,72,128]{2,1,0:T(8,128)(2,1)} %copy.47.r_ref, s32[16,128]{1,0:T(8,128)} %pad.9.t_ref), custom_call_target="tpu_custom_call" | custom-call | tf_op jit(solution)/shard_map/pallas_call | solution.py:362
  23.3 19.1 %shard_map.65 = (f32[256,128]{1,0:T(8,128)}, bf16[64,128,128]{2,1,0:T(8,128)(2,1)}) custom-call(s32[64,4]{1,0:T(8,128)} %bitcast.26, bf16[4,6,72,128]{3,2,1,0:T(8,128)(2,1)} %get-tuple-element.11.wall, bf16[8,2,72,128]{3,2,1,0:T(8,128)(2,1)} %get-tuple-element.12.rall), custom_call_target="tpu_custom_call" | custom-call | tf_op jit(solution)/shard_map/pallas_call | solution.py:387
  42.4 9.0 %shard_map.66.parts = f32[4,256,128]{2,1,0:T(8,128)} custom-call(f32[256,128]{1,0:T(8,128)} %get-tuple-element.13.x_ref), custom_call_target="tpu_custom_call" | custom-call | tf_op jit(solution)/shard_map/pallas_call | solution.py:114
  51.4 16.0 %shard_map.67.x_ref = bf16[8,3,72,128]{3,2,1,0:T(8,128)(2,1)} custom-call(s32[64,4]{1,0:T(8,128)} %bitcast.27, f32[4,256,128]{2,1,0:T(8,128)} %shard_map.66.parts, bf16[64,128,128]{2,1,0:T(8,128)(2,1)} %get-tuple-element.14.weights_ref), custom_call_target="tpu_custom_call" | custom-call | tf_op jit(solution)/shard_map/pallas_call | solution.py:402
  67.4 14.9 %shard_map.68 = f32[3,72,128]{2,1,0:T(8,128)} custom-call(bf16[8,3,72,128]{3,2,1,0:T(8,128)(2,1)} %shard_map.67.x_ref), custom_call_target="tpu_custom_call" | custom-call | tf_op jit(solution)/shard_map/pallas_call | solution.py:415
  82.3 0.8 slice.19
  83.0 0.9 %slice.17 = f32[2,72,128]{2,1,0:T(8,128)S(1)} slice(f32[3,72,128]{2,1,0:T(8,128)} %shard_map.68), slice={[0:2], [0:72], [0:128]} | slice | bytes 147456 | tf_op jit(solution)/shard_map/slice | solution.py:428
  83.9 0.1 copy.49
  84.0 0.1 copy.48
  84.2 0.8 reshape.78
  (15 shorter events, 0.3 us)
Async XLA Ops:
  0.0 2.4 %copy-start = (bf16[7,9216]{1,0:T(8,128)(2,1)S(1)}, bf16[7,9216]{1,0:T(8,128)(2,1)}, u32[]{:S(2)}) copy-start(bf16[7,9216]{1,0:T(8,128)(2,1)} %param.10) | copy-start | bytes 387076
  0.0 5.2 %copy-start.1 = (bf16[16,4608]{1,0:T(8,128)(2,1)S(1)}, bf16[16,4608]{1,0:T(8,128)(2,1)}, u32[]{:S(2)}) copy-start(bf16[16,4608]{1,0:T(8,128)(2,1)} %param.7) | copy-start | bytes 442372
  0.0 5.7 %copy-start.2 = (bf16[16,9216]{1,0:T(8,128)(2,1)S(1)}, bf16[16,9216]{1,0:T(8,128)(2,1)}, u32[]{:S(2)}) copy-start(bf16[16,9216]{1,0:T(8,128)(2,1)} %param.6) | copy-start | bytes 884740
where the time goes:
time: 86.4 us; the launch traced here: 85.1 us
  Pallas kernels  73.1 us (85%)
  local copies, waits for them, and re-layouts  8.92 us (10%)
  other arithmetic  2.85 us (3%)
    pallas_call x1, Pallas kernels, on_device(): pl.pallas_call(functools.partial(score_kernel, dims), out_shape=(jax.Shap...  19.1 us
    pallas_call x1, Pallas kernels, on_device(): pl.pallas_call(functools.partial(total_kernel, dims), out_shape=jax.Shape...  16 us
    pallas_call x1, Pallas kernels, on_device(): pl.pallas_call(functools.partial(gather_kernel, 'cls', owners), out_shape...  14.9 us
    pallas_call x1, Pallas kernels, on_device(): pl.pallas_call(functools.partial(spread_kernel, owners, fellows), out_sha...  14.2 us
    pallas_call x1, Pallas kernels, exchange(): pl.pallas_call(functools.partial(exchange_kernel, axis, size, split=split...  9.05 us
    reshape x1, local copies, waits for them, and re-layouts, on_device(): images.astype(F32).reshape(particles, shells, 2, angles)  2.15 us
    reshape x2, local copies, waits for them, and re-layouts, on_device(): ctf.astype(F32).reshape(particles, shells, angles)  1.89 us

commit v1 on v0

--- a/solution.py
+++ b/solution.py
@@ -30,101 +30,6 @@
     pl.semaphore_wait(barrier, total)
 
 
-def spread_kernel(owners, fellows, w_ref, r_ref, t_ref, wall, rall, tall, own_sem, ws, wr, rs, rr, ts, tr):
-    my_owner = lax.axis_index("cls")
-    my_fellow = lax.axis_index("img")
-    greet((("cls", owners), ("img", fellows)))
-    copies = []
-    for step in range(1, owners):
-        peer = lax.rem(my_owner + step, owners)
-        copies.append(
-            pltpu.make_async_remote_copy(
-                src_ref=r_ref,
-                dst_ref=rall.at[my_owner],
-                send_sem=rs.at[step],
-                recv_sem=rr.at[step],
-                device_id={"cls": peer},
-                device_id_type=MESH,
-            )
-        )
-    for step in range(1, fellows):
-        peer = lax.rem(my_fellow + step, fellows)
-        copies.append(
-            pltpu.make_async_remote_copy(
-                src_ref=t_ref,
-                dst_ref=tall.at[my_fellow],
-                send_sem=ts.at[step],
-                recv_sem=tr.at[step],
-                device_id={"img": peer},
-                device_id_type=MESH,
-            )
-        )
-        copies.append(
-            pltpu.make_async_remote_copy(
-                src_ref=w_ref.at[peer],
-                dst_ref=wall.at[my_fellow],
-                send_sem=ws.at[step],
-                recv_sem=wr.at[step],
-                device_id={"img": peer},
-                device_id_type=MESH,
-            )
-        )
-    for copy in copies:
-        copy.start()
-    own = [
-        pltpu.make_async_copy(w_ref.at[my_fellow], wall.at[my_fellow], own_sem.at[0]),
-        pltpu.make_async_copy(r_ref, rall.at[my_owner], own_sem.at[1]),
-        pltpu.make_async_copy(t_ref, tall.at[my_fellow], own_sem.at[2]),
-    ]
-    for copy in own:
-        copy.start()
-    for copy in own:
-        copy.wait()
-    for copy in copies:
-        copy.wait()
-
-
-def exchange_kernel(axis, size, x_ref, out_ref, own_sem, send, recv, *, split):
-    me = lax.axis_index(axis)
-    greet(((axis, size),))
-    copies = []
-    for step in range(1, size):
-        peer = lax.rem(me + step, size)
-        copies.append(
-            pltpu.make_async_remote_copy(
-                src_ref=x_ref.at[peer] if split else x_ref,
-                dst_ref=out_ref.at[me],
-                send_sem=send.at[step],
-                recv_sem=recv.at[step],
-                device_id={axis: peer},
-                device_id_type=MESH,
-            )
-        )
-    for copy in copies:
-        copy.start()
-    own = pltpu.make_async_copy(x_ref.at[me] if split else x_ref, out_ref.at[me], own_sem.at[0])
-    own.start()
-    own.wait()
-    for copy in copies:
-        copy.wait()
-
-
-def exchange(x, axis, size, split, collective_id):
-    block = x.shape[1:] if split else x.shape
-    return pl.pallas_call(
-        functools.partial(exchange_kernel, axis, size, split=split),
-        out_shape=jax.ShapeDtypeStruct((size,) + block, x.dtype),
-        in_specs=vmem_specs(1),
-        out_specs=pl.BlockSpec(memory_space=pltpu.VMEM),
-        scratch_shapes=[
-            pltpu.SemaphoreType.DMA((1,)),
-            pltpu.SemaphoreType.DMA((size,)),
-            pltpu.SemaphoreType.DMA((size,)),
-        ],
-        compiler_params=pltpu.CompilerParams(collective_id=collective_id, has_side_effects=True),
-    )(x)
-
-
 def lane_of(shape):
     return lax.broadcasted_iota(jnp.int32, shape, len(shape) - 1)
 
@@ -133,31 +38,70 @@
     return pltpu.roll(x, shift % LANES, x.ndim - 1)
 
 
-def score_kernel(dims, rows_ref, wall, rall, logits_ref, weights_ref, table, low, high):
+def score_kernel(
+    dims, w_ref, r_ref, t_ref, parts, weights_ref, tall, wall, rall, rows_ref, table, low, high,
+    own_sem, ws, wr, rs, rr, ts, tr, ls, lr,
+):
     fellows, particles, owners, slots, top, angles, half = dims
     width = 2 * half
     per_pack = LANES // width
     per_den = LANES // half
     tall_rows = table.shape[1]
     num_packs = particles // per_pack
+    tiles = angles // 8
+    cut = (tiles // 2 + tiles % 2) * 8
+    my_owner = lax.axis_index("cls")
+    my_fellow = lax.axis_index("img")
+    greet((("cls", owners), ("img", fellows)))
+
+    def remote(src, dst, send, recv, axis, peer):
+        return pltpu.make_async_remote_copy(
+            src_ref=src,
+            dst_ref=dst,
+            send_sem=send,
+            recv_sem=recv,
+            device_id={axis: peer},
+            device_id_type=MESH,
+        )
+
+    row_copies = []
+    ref_copies = []
+    image_copies = []
+    for step in range(1, fellows):
+        peer = lax.rem(my_fellow + step, fellows)
+        row_copies.append(remote(t_ref, tall.at[my_fellow], ts.at[step], tr.at[step], "img", peer))
+        image_copies.append(
+            remote(w_ref.at[peer], wall.at[my_fellow], ws.at[step], wr.at[step], "img", peer)
+        )
+    for step in range(1, owners):
+        peer = lax.rem(my_owner + step, owners)
+        ref_copies.append(remote(r_ref, rall.at[my_owner], rs.at[step], rr.at[step], "cls", peer))
+    for copy in row_copies + ref_copies + image_copies:
+        copy.start()
+    own_rows = pltpu.make_async_copy(t_ref, tall.at[my_fellow], own_sem.at[0])
+    own_rows.start()
+
     lane = lane_of((angles, LANES))
     zero_tail = jnp.zeros((LANES - angles, LANES), F32)
 
-    def place(fellow, carry):
-        for i in range(particles):
-            num = wall[fellow, i // per_pack].astype(F32)
-            den = wall[fellow, num_packs + i // per_den].astype(F32)
-            num = roll(num, -width * (i % per_pack))
-            den = roll(den, width - half * (i % per_den))
-            joined = jnp.where(lane < width, num, jnp.where(lane < width + half, den, 0.0))
-            weights_ref[fellow * particles + i] = jnp.concatenate([joined, zero_tail], axis=0).astype(BF16)
-        return carry
-
-    lax.fori_loop(0, fellows, place, 0)
-
-    def tabulate(owner, carry):
+    def place(fellow, read):
+        def some(u, carry):
+            for g in range(per_den):
+                num = read(u * (per_den // per_pack) + g // per_pack).astype(F32)
+                den = read(num_packs + u).astype(F32)
+                num = roll(num, -width * (g % per_pack))
+                den = roll(den, width - half * g)
+                joined = jnp.where(lane < width, num, jnp.where(lane < width + half, den, 0.0))
+                weights_ref[fellow * particles + u * per_den + g] = jnp.concatenate(
+                    [joined, zero_tail], axis=0
+                ).astype(BF16)
+            return carry
+
+        lax.fori_loop(0, particles // per_den, some, 0)
+
+    def tabulate(owner, read):
         for t in range(slots):
-            ref = roll(rall[owner, t // per_pack].astype(F32), -width * (t % per_pack))
+            ref = roll(read(t // per_pack).astype(F32), -width * (t % per_pack))
             square = ref * ref
             power = (square + roll(square, -half)).astype(BF16).astype(F32) * -0.5
             power = roll(power, width)
@@ -165,20 +109,38 @@
             table[owner * slots + t] = jnp.concatenate(
                 [joined, jnp.zeros((tall_rows - angles, LANES), F32)], axis=0
             ).astype(BF16)
-        return carry
-
-    lax.fori_loop(0, owners, tabulate, 0)
-    cut = (angles // 16) * 8 + (8 if (angles // 8) % 2 else 0)
-    tiles = angles // 8
-
-    def pair(m, carry):
+
+    place(my_fellow, lambda u: w_ref[my_fellow, u])
+    tabulate(my_owner, lambda u: r_ref[u])
+    own_rows.wait()
+    for copy in row_copies:
+        copy.wait_recv()
+    to_smem = pltpu.make_async_copy(tall, rows_ref, own_sem.at[1])
+    to_smem.start()
+    for step in range(1, max(owners, fellows)):
+        if step < fellows:
+            image_copies[step - 1].wait_recv()
+            source = lax.rem(my_fellow + fellows - step, fellows)
+            place(source, lambda u: wall[source, u])
+        if step < owners:
+            ref_copies[step - 1].wait_recv()
+            holder = lax.rem(my_owner + owners - step, owners)
+            tabulate(holder, lambda u: rall[holder, u])
+    to_smem.wait()
+
+    batch = 8
+
+    def score(fellow, begin):
         lows = []
         highs = []
-        for k in range(2):
-            i = 2 * m + k
-            refs = jnp.concatenate([table[rows_ref[i, j]] for j in range(top)], axis=0)
+        for k in range(batch):
+            i = begin + k
+            refs = jnp.concatenate([table[rows_ref[fellow, i, j]] for j in range(top)], axis=0)
             grid = lax.dot_general(
-                refs, weights_ref[i], (((1,), (1,)), ((), ())), preferred_element_type=F32
+                refs,
+                weights_ref[fellow * particles + i],
+                (((1,), (1,)), ((), ())),
+                preferred_element_type=F32,
             )
             for j in range(top):
                 base = j * tall_rows
@@ -192,18 +154,37 @@
                 hi = pltpu.roll(hi, 0, 1, stride=1, stride_axis=0)
                 lows.append(jnp.sum(lo, axis=0, keepdims=True))
                 highs.append(jnp.sum(hi, axis=0, keepdims=True))
-        low[m] = jnp.concatenate(lows, axis=0)
-        high[m] = jnp.concatenate(highs, axis=0)
-        return carry
-
-    lax.fori_loop(0, low.shape[0], pair, 0)
-    lo = low[...].reshape(-1, LANES)
-    hi = high[...].reshape(-1, LANES)
-    spot = lane_of(lo.shape)
-    total = roll(lo, 1) + jnp.where(spot < cut, roll(lo, 1 - angles), 0.0)
-    back = angles - 1 - cut
-    total = total + roll(hi, -back) + jnp.where(spot >= cut + 1, roll(hi, cut + 1), 0.0)
-    logits_ref[...] = jnp.where(spot < angles, total, 0.0)
+        rows = batch * top
+        start = pl.multiple_of(begin * top, rows)
+        low[pl.ds(start, rows)] = jnp.concatenate(lows, axis=0)
+        high[pl.ds(start, rows)] = jnp.concatenate(highs, axis=0)
+
+    part_copies = []
+    chunk = particles * top
+    for fellow in range(fellows):
+
+        def some(b, carry):
+            score(fellow, b * batch)
+            return carry
+
+        lax.fori_loop(0, particles // batch, some, 0)
+        lo = low[...]
+        hi = high[...]
+        spot = lane_of(lo.shape)
+        total = roll(lo, 1) + jnp.where(spot < cut, roll(lo, 1 - angles), 0.0)
+        back = angles - 1 - cut
+        total = total + roll(hi, -back) + jnp.where(spot >= cut + 1, roll(hi, cut + 1), 0.0)
+        place_at = parts.at[my_fellow, pl.ds(fellow * chunk, chunk)]
+        parts[my_fellow, pl.ds(fellow * chunk, chunk)] = jnp.where(spot < angles, total, 0.0)
+        for step in range(1, fellows):
+            peer = lax.rem(my_fellow + step, fellows)
+            copy = remote(place_at, place_at, ls.at[step, fellow], lr.at[step, fellow], "img", peer)
+            copy.start()
+            part_copies.append(copy)
+    for copy in row_copies + ref_copies + image_copies:
+        copy.wait_send()
+    for copy in part_copies:
+        copy.wait()
 
 
 def group_of(x, top, combine):
@@ -245,7 +226,7 @@
     ext_hi[...] = hi.reshape(ext_hi.shape)
     acc[...] = jnp.zeros_like(acc)
 
-    def pair(m, carry):
+    def pair(m):
         lo_rows = ext_lo[m]
         hi_rows = ext_hi[m]
         for k in range(2):
@@ -269,12 +250,17 @@
                     turned.append(second)
             circle = jnp.concatenate(turned, axis=0).astype(BF16)
             grid = jnp.dot(circle, weights_ref[i], preferred_element_type=F32)
+            held = [acc[rows_ref[i, j]] for j in range(top)]
             for j in range(top):
-                row = rows_ref[i, j]
-                acc[row] = acc[row] + grid[j * tall_rows : j * tall_rows + angles]
+                acc[rows_ref[i, j]] = held[j] + grid[j * tall_rows : j * tall_rows + angles]
+
+    def some(b, carry):
+        for m in range(batch // 2):
+            pair(b * (batch // 2) + m)
         return carry
 
-    lax.fori_loop(0, ext_lo.shape[0], pair, 0)
+    batch = 8
+    lax.fori_loop(0, ext_lo.shape[0] // (batch // 2), some, 0)
     lane = lane_of((angles, LANES))
 
     def pack(owner, carry):
@@ -359,46 +345,40 @@
     rows = jnp.pad(rows, ((0, 0), (0, LANES - top)))
 
     packs = send.shape[1]
-    wall, rall, tall = pl.pallas_call(
-        functools.partial(spread_kernel, owners, fellows),
+    everyone = fellows * particles
+    tall_rows = -(-angles // 16) * 16
+    pairs = everyone // 2
+    smem = pl.BlockSpec(memory_space=pltpu.SMEM)
+    dma = pltpu.SemaphoreType.DMA
+    parts, weights, tall = pl.pallas_call(
+        functools.partial(score_kernel, dims),
         out_shape=(
-            jax.ShapeDtypeStruct((fellows, packs, angles, LANES), BF16),
-            jax.ShapeDtypeStruct((owners,) + mine.shape, BF16),
+            jax.ShapeDtypeStruct((fellows, everyone * top, LANES), F32),
+            jax.ShapeDtypeStruct((everyone, LANES, LANES), BF16),
             jax.ShapeDtypeStruct((fellows, particles, LANES), jnp.int32),
         ),
         in_specs=vmem_specs(3),
         out_specs=tuple(vmem_specs(3)),
         scratch_shapes=[
-            pltpu.SemaphoreType.DMA((3,)),
-            pltpu.SemaphoreType.DMA((fellows,)),
-            pltpu.SemaphoreType.DMA((fellows,)),
-            pltpu.SemaphoreType.DMA((owners,)),
-            pltpu.SemaphoreType.DMA((owners,)),
-            pltpu.SemaphoreType.DMA((fellows,)),
-            pltpu.SemaphoreType.DMA((fellows,)),
+            VMEM((fellows, packs, angles, LANES), BF16),
+            VMEM((owners,) + mine.shape, BF16),
+            pltpu.SMEM((fellows, particles, LANES), jnp.int32),
+            VMEM((owners * slots, tall_rows, LANES), BF16),
+            VMEM((particles * top, LANES), F32),
+            VMEM((particles * top, LANES), F32),
+            dma((2,)),
+            dma((fellows,)),
+            dma((fellows,)),
+            dma((owners,)),
+            dma((owners,)),
+            dma((fellows,)),
+            dma((fellows,)),
+            dma((fellows, fellows)),
+            dma((fellows, fellows)),
         ],
         compiler_params=pltpu.CompilerParams(collective_id=0, has_side_effects=True),
     )(send, mine, rows)
-    everyone = fellows * particles
     row_list = tall[:, :, :top].reshape(everyone, top)
-    tall_rows = -(-angles // 16) * 16
-    pairs = everyone // 2
-    smem = pl.BlockSpec(memory_space=pltpu.SMEM)
-    logits, weights = pl.pallas_call(
-        functools.partial(score_kernel, dims),
-        out_shape=(
-            jax.ShapeDtypeStruct((everyone * top, LANES), F32),
-            jax.ShapeDtypeStruct((everyone, LANES, LANES), BF16),
-        ),
-        in_specs=[smem] + vmem_specs(2),
-        out_specs=tuple(vmem_specs(2)),
-        scratch_shapes=[
-            VMEM((owners * slots, tall_rows, LANES), BF16),
-            VMEM((pairs, 2 * top, LANES), F32),
-            VMEM((pairs, 2 * top, LANES), F32),
-        ],
-    )(row_list, wall, rall)
-    parts = exchange(logits, "img", fellows, False, 1)
     sums = pl.pallas_call(
         functools.partial(total_kernel, dims),
         out_shape=jax.ShapeDtypeStruct(

time: 86.4 us -> 62 us (0.72); the launches traced: 85.1 us -> 61.6 us
  Pallas kernels: 73.1 us -> 49.7 us
    pallas_call x2 -> x0, Pallas kernels: 23.2 us -> none  [the longest x1 14.2 us: on_device(): pl.pallas_call(functools.partial(spread_kernel, owners, fellows), out_sha...]
    pallas_call x1, Pallas kernels: 19.1 us -> 26.8 us  [on_device(): pl.pallas_call(functools.partial(score_kernel, dims), out_shape=(jax.Shap...]
    pallas_call x1, Pallas kernels: 16 us -> 9.45 us  [on_device(): pl.pallas_call(functools.partial(total_kernel, dims), out_shape=jax.Shape...]
    pallas_call x1, Pallas kernels: 14.9 us -> 13.5 us  [on_device(): pl.pallas_call(functools.partial(gather_kernel, 'cls', owners), out_shape...]
where the time goes in v1:
time: 62 us; the launch traced here: 61.6 us
  Pallas kernels  49.7 us (80%)
  local copies, waits for them, and re-layouts  8.92 us (14%)
  other arithmetic  2.88 us (5%)
    pallas_call x1, Pallas kernels, on_device(): pl.pallas_call(functools.partial(score_kernel, dims), out_shape=(jax.Shap...  26.8 us
    pallas_call x1, Pallas kernels, on_device(): pl.pallas_call(functools.partial(gather_kernel, 'cls', owners), out_shape...  13.5 us
    pallas_call x1, Pallas kernels, on_device(): pl.pallas_call(functools.partial(total_kernel, dims), out_shape=jax.Shape...  9.45 us
    reshape x1, local copies, waits for them, and re-layouts, on_device(): images.astype(F32).reshape(particles, shells, 2, angles)  2.15 us
    reshape x2, local copies, waits for them, and re-layouts, on_device(): ctf.astype(F32).reshape(particles, shells, angles)  1.89 us

profile of v1, /device:TPU:0, one launch (start us, length us, event | category | flops | bytes accessed | tf_op | source)
XLA Modules:
  0.0 61.6 jit_solution(14035752767650662596)
XLA Ops:
  0.0 0.7 %broadcast_divide_fusion = f32[64]{0:T(128)S(1)} fusion(f32[64]{0:T(128)} %param.11), kind=kLoop, calls=%fused_computation.19 | loop fusion | flops 64 | bytes 512 | tf_op jit(solution)/shard_map/div | solution.py:327
  0.7 0.1 mul.41
  0.8 0.9 %select_reduce_fusion = s32[16,4]{0,1:T(4,128)S(1)} fusion(s32[56]{0:T(128)} %param.9, s32[16,4]{0,1:T(4,128)} %param.8), kind=kLoop, calls=%fused_computation.9 | loop fusion | flops 10688 | bytes 736 | tf_op jit(solution)/shard_map/reduce_sum | solution.py:343
  1.7 0.1 copy.44
  1.8 0.6 pad.9.t_ref
  2.5 0.2 reshape.72
  2.6 0.1 rev.3
  2.7 0.7 %copy.47.r_ref = bf16[2,72,128]{2,1,0:T(8,128)(2,1)} copy(bf16[2,72,128]{1,2,0:T(8,128)(2,1)S(1)} %bitcast.24) | data formatting | bytes 73728 | tf_op jit(solution)/shard_map/reshape | solution.py:340
  3.5 1.4 %reshape.70 = f32[2,8,4,16,72]{4,3,2,1,0:T(8,128)S(1)} reshape(bf16[16,4608]{1,0:T(8,128)(2,1)} %param.7) | data formatting | bytes 442368 | tf_op jit(solution)/shard_map/reshape | solution.py:327
  4.9 0.1 fusion.1
  5.0 0.1 copy.42
  5.2 0.5 reshape.68
  5.7 2.1 %reshape.80 = f32[4,4,4,16,2,72]{5,4,3,2,1,0:T(2,128)S(1)} reshape(bf16[16,9216]{1,0:T(8,128)(2,1)S(1)} %copy-done.2) | data formatting | bytes 884736 | tf_op jit(solution)/shard_map/reshape | solution.py:329
  7.8 0.2 fusion
  8.1 0.2 copy.41
  8.3 0.8 %pad_maximum_fusion.w_ref = bf16[4,6,72,128]{3,2,1,0:T(8,128)(2,1)} fusion(bf16[4,2,72,128]{3,2,1,0:T(8,128)(2,1)S(1)} %copy.42, bf16[4,4,72,128]{3,2,1,0:T(8,128)(2,1)S(1)} %copy.41), kind=kLoop, calls=%fused_computation.4 | loop fusion | flops 221184 | bytes 884736 | tf_op jit(solution)/shard_map/concatenate | solution.py:336
  9.1 26.8 %shard_map.64 = (f32[4,256,128]{2,1,0:T(8,128)}, bf16[64,128,128]{2,1,0:T(8,128)(2,1)}, s32[4,16,128]{2,1,0:T(8,128)}) custom-call(bf16[4,6,72,128]{3,2,1,0:T(8,128)(2,1)} %pad_maximum_fusion.w_ref, bf16[2,72,128]{2,1,0:T(8,128)(2,1)} %copy.47.r_ref, s32[16,128]{1,0:T(8,128)} %pad.9.t_ref), custom_call_target="tpu_custom_call" | custom-call | tf_op jit(solution)/shard_map/pallas_call | solution.py:353
  35.9 9.5 %shard_map.65.x_ref = bf16[8,3,72,128]{3,2,1,0:T(8,128)(2,1)} custom-call(s32[64,4]{1,0:T(8,128)} %bitcast.26, f32[4,256,128]{2,1,0:T(8,128)} %get-tuple-element.9.parts, bf16[64,128,128]{2,1,0:T(8,128)(2,1)} %get-tuple-element.10.weights_ref), custom_call_target="tpu_custom_call" | custom-call | tf_op jit(solution)/shard_map/pallas_call | solution.py:382
  45.4 13.5 %shard_map.66 = f32[3,72,128]{2,1,0:T(8,128)} custom-call(bf16[8,3,72,128]{3,2,1,0:T(8,128)(2,1)} %shard_map.65.x_ref), custom_call_target="tpu_custom_call" | custom-call | tf_op jit(solution)/shard_map/pallas_call | solution.py:395
  58.9 0.8 %slice.19 = f32[1,72,128]{2,1,0:T(8,128)S(1)} slice(f32[3,72,128]{2,1,0:T(8,128)} %shard_map.66), slice={[2:3], [0:72], [0:128]} | slice | bytes 73728 | tf_op jit(solution)/shard_map/slice | solution.py:410
  59.6 0.9 %slice.17 = f32[2,72,128]{2,1,0:T(8,128)S(1)} slice(f32[3,72,128]{2,1,0:T(8,128)} %shard_map.66), slice={[0:2], [0:72], [0:128]} | slice | bytes 147456 | tf_op jit(solution)/shard_map/slice | solution.py:408
  60.5 0.1 copy.49
  60.6 0.1 copy.48
  60.8 0.8 %reshape.78 = f32[7,2304]{1,0:T(8,128)} reshape(f32[7,16,2,72]{3,2,1,0:T(2,128)S(1)} %copy.50) | data formatting | bytes 129024 | tf_op jit(solution)/shard_map/reshape | solution.py:412
  (13 shorter events, 0.1 us)
Async XLA Ops:
  0.0 2.4 %copy-start = (bf16[7,9216]{1,0:T(8,128)(2,1)S(1)}, bf16[7,9216]{1,0:T(8,128)(2,1)}, u32[]{:S(2)}) copy-start(bf16[7,9216]{1,0:T(8,128)(2,1)} %param.10) | copy-start | bytes 387076
  0.0 5.2 %copy-start.1 = (bf16[16,4608]{1,0:T(8,128)(2,1)S(1)}, bf16[16,4608]{1,0:T(8,128)(2,1)}, u32[]{:S(2)}) copy-start(bf16[16,4608]{1,0:T(8,128)(2,1)} %param.7) | copy-start | bytes 442372
  0.0 5.7 %copy-start.2 = (bf16[16,9216]{1,0:T(8,128)(2,1)S(1)}, bf16[16,9216]{1,0:T(8,128)(2,1)}, u32[]{:S(2)}) copy-start(bf16[16,9216]{1,0:T(8,128)(2,1)} %param.6) | copy-start | bytes 884740

commit v2 on v1

--- a/solution.py
+++ b/solution.py
@@ -39,10 +39,11 @@
 
 
 def score_kernel(
-    dims, w_ref, r_ref, t_ref, parts, weights_ref, tall, wall, rall, rows_ref, table, low, high,
+    dims, place_ref, w_ref, r_ref, t_ref, sigma_ref, parts, weights_ref, tall, wall, rall, rows_ref,
+    table, low, high, pick_num, pick_den,
     own_sem, ws, wr, rs, rr, ts, tr, ls, lr,
 ):
-    fellows, particles, owners, slots, top, angles, half = dims
+    fellows, particles, owners, per_owner, slots, top, angles, half = dims
     width = 2 * half
     per_pack = LANES // width
     per_den = LANES // half
@@ -83,15 +84,34 @@
 
     lane = lane_of((angles, LANES))
     zero_tail = jnp.zeros((LANES - angles, LANES), F32)
+    source_lane = lax.broadcasted_iota(jnp.int32, (LANES, LANES), 0)
+    target_lane = lax.broadcasted_iota(jnp.int32, (LANES, LANES), 1)
+    shell = target_lane % half
+    num_source = jnp.where(target_lane < width, 2 * shell + target_lane // half, -LANES)
+    for g in range(per_pack):
+        pick_num[g] = (source_lane == num_source + width * g).astype(F32).astype(BF16)
+    den_source = jnp.where(target_lane < width + half, shell, -LANES)
+    for g in range(per_den):
+        pick_den[g] = (source_lane == den_source + half * g).astype(F32).astype(BF16)
+    spread = jnp.concatenate([1.0 / sigma_ref[...]] * (LANES // sigma_ref.shape[1]), axis=1)
+    spread = jnp.broadcast_to(spread, (8, LANES))
+    row_lane = lane_of((8, LANES))
+    inverse = jnp.zeros((8, LANES), F32)
+    for part in range(3):
+        shift = lax.rem(half * part - half * my_fellow + LANES, LANES)
+        inverse = jnp.where(row_lane // half == part, pltpu.roll(spread, shift, 1), inverse)
+    inverse = inverse[0:1]
 
     def place(fellow, read):
         def some(u, carry):
             for g in range(per_den):
-                num = read(u * (per_den // per_pack) + g // per_pack).astype(F32)
-                den = read(num_packs + u).astype(F32)
-                num = roll(num, -width * (g % per_pack))
-                den = roll(den, width - half * g)
-                joined = jnp.where(lane < width, num, jnp.where(lane < width + half, den, 0.0))
+                num = jnp.dot(
+                    read(u * (per_den // per_pack) + g // per_pack),
+                    pick_num[g % per_pack],
+                    preferred_element_type=F32,
+                )
+                den = jnp.dot(read(num_packs + u), pick_den[g], preferred_element_type=F32)
+                joined = jnp.where(lane < width, num, den) * (den * inverse)
                 weights_ref[fellow * particles + u * per_den + g] = jnp.concatenate(
                     [joined, zero_tail], axis=0
                 ).astype(BF16)
@@ -100,13 +120,13 @@
         lax.fori_loop(0, particles // per_den, some, 0)
 
     def tabulate(owner, read):
-        for t in range(slots):
-            ref = roll(read(t // per_pack).astype(F32), -width * (t % per_pack))
+        for t in range(per_owner):
+            ref = jnp.dot(read(t // per_pack), pick_num[t % per_pack], preferred_element_type=F32)
             square = ref * ref
             power = (square + roll(square, -half)).astype(BF16).astype(F32) * -0.5
             power = roll(power, width)
             joined = jnp.where(lane < width, ref, jnp.where(lane < width + half, power, 0.0))
-            table[owner * slots + t] = jnp.concatenate(
+            table[owner * per_owner + t] = jnp.concatenate(
                 [joined, jnp.zeros((tall_rows - angles, LANES), F32)], axis=0
             ).astype(BF16)
 
@@ -135,7 +155,7 @@
         highs = []
         for k in range(batch):
             i = begin + k
-            refs = jnp.concatenate([table[rows_ref[fellow, i, j]] for j in range(top)], axis=0)
+            refs = jnp.concatenate([table[place_ref[rows_ref[fellow, i, j]]] for j in range(top)], axis=0)
             grid = lax.dot_general(
                 refs,
                 weights_ref[fellow * particles + i],
@@ -200,8 +220,8 @@
     return x
 
 
-def total_kernel(dims, rows_ref, parts, weights_ref, out_ref, acc, ext_lo, ext_hi):
-    fellows, particles, owners, slots, top, angles, half = dims
+def total_kernel(dims, place_ref, rows_ref, parts, weights_ref, out_ref, acc, ext_lo, ext_hi):
+    fellows, particles, owners, per_owner, slots, top, angles, half = dims
     width = 2 * half
     per_pack = LANES // width
     per_den = LANES // half
@@ -250,9 +270,10 @@
                     turned.append(second)
             circle = jnp.concatenate(turned, axis=0).astype(BF16)
             grid = jnp.dot(circle, weights_ref[i], preferred_element_type=F32)
-            held = [acc[rows_ref[i, j]] for j in range(top)]
+            spots = [place_ref[rows_ref[i, j]] for j in range(top)]
+            held = [acc[spot] for spot in spots]
             for j in range(top):
-                acc[rows_ref[i, j]] = held[j] + grid[j * tall_rows : j * tall_rows + angles]
+                acc[spots[j]] = held[j] + grid[j * tall_rows : j * tall_rows + angles]
 
     def some(b, carry):
         for m in range(batch // 2):
@@ -265,9 +286,9 @@
 
     def pack(owner, carry):
         nums = [None] * num_packs
-        dens = [None] * (slots // per_den)
-        for t in range(slots):
-            value = acc[owner * slots + t]
+        dens = [None] * -(-slots // per_den)
+        for t in range(per_owner):
+            value = acc[owner * per_owner + t]
             g, u = t % per_pack, t // per_pack
             num = roll(value, width * g)
             nums[u] = num if g == 0 else jnp.where(lane >= width * g, num, nums[u])
@@ -281,7 +302,7 @@
     lax.fori_loop(0, owners, pack, 0)
 
 
-def gather_kernel(axis, size, x_ref, out_ref, landed, send, recv):
+def gather_kernel(axis, size, half, slots, x_ref, out_ref, landed, send, recv):
     me = lax.axis_index(axis)
     greet(((axis, size),))
     copies = []
@@ -303,7 +324,28 @@
     for step in range(1, size):
         copies[step - 1].wait_recv()
         total = total + landed[step - 1].astype(F32)
-    out_ref[...] = total
+    width = 2 * half
+    per_pack = LANES // width
+    num_packs = slots // per_pack
+    target = lax.broadcasted_iota(jnp.int32, (LANES, LANES), 0)
+    source = lax.broadcasted_iota(jnp.int32, (LANES, LANES), 1)
+    shell = (target % width) // 2
+    flip = target - target % width + (target % 2) * half + shell
+
+    def picked(wanted, x):
+        return lax.dot_general(
+            (source == wanted).astype(F32),
+            x,
+            (((1,), (1,)), ((), ())),
+            precision=lax.Precision.HIGHEST,
+            preferred_element_type=F32,
+        )
+
+    for u in range(num_packs):
+        held = num_packs + (u * per_pack * half) // LANES
+        offset = (u * per_pack * half) % LANES
+        den = picked(offset + half * (target // width) + shell, total[held])
+        out_ref[u] = picked(flip, total[u]) / (den + 1.0)
     for copy in copies:
         copy.wait_send()
 
@@ -321,28 +363,19 @@
     width = 2 * half
     per_pack = LANES // width
     per_den = LANES // half
-    slots = -(-per_owner // per_den) * per_den
-    dims = (fellows, particles, owners, slots, top, angles, half)
-
-    scaling = ctf.astype(F32).reshape(particles, shells, angles) * (1.0 / sigma2)[None, :, None]
-    weighted = (
-        images.astype(F32).reshape(particles, shells, 2, angles) * scaling[:, :, None, :]
-    ).astype(BF16)
-    ctf_power = (ctf.astype(F32).reshape(particles, shells, angles) * scaling).astype(BF16)
-    num = weighted.reshape(particles // per_pack, per_pack, fellows, half, 2, angles)
-    num = num.transpose(2, 0, 5, 1, 4, 3).reshape(fellows, -1, angles, LANES)
-    den = ctf_power.reshape(particles // per_den, per_den, fellows, half, angles)
+    slots = -(-per_owner // per_pack) * per_pack
+    dims = (fellows, particles, owners, per_owner, slots, top, angles, half)
+
+    num = images.reshape(particles // per_pack, per_pack, fellows, width, angles)
+    num = num.transpose(2, 0, 4, 1, 3).reshape(fellows, -1, angles, LANES)
+    den = ctf.reshape(particles // per_den, per_den, fellows, half, angles)
     den = den.transpose(2, 0, 4, 1, 3).reshape(fellows, -1, angles, LANES)
     send = jnp.concatenate([num, den], axis=1)
     mine = lax.dynamic_slice_in_dim(references, my_fellow * (width * angles), width * angles, 1)
     mine = jnp.pad(mine, ((0, slots - per_owner), (0, 0)))
-    mine = mine.reshape(slots // per_pack, per_pack, half, 2, angles)[..., ::-1]
-    mine = mine.transpose(0, 4, 1, 3, 2).reshape(-1, angles, LANES)
-
-    lookup = classes[:, :, None] == jnp.arange(class_place.shape[0], dtype=jnp.int32)[None, None, :]
-    table_rows = jnp.sum(jnp.where(lookup, class_place[None, None, :], 0), axis=2)
-    rows = (table_rows // per_owner) * slots + table_rows % per_owner
-    rows = jnp.pad(rows, ((0, 0), (0, LANES - top)))
+    mine = mine.reshape(slots // per_pack, per_pack, width, angles)[..., ::-1]
+    mine = mine.transpose(0, 3, 1, 2).reshape(-1, angles, LANES)
+    rows = jnp.pad(classes, ((0, 0), (0, LANES - top)))
 
     packs = send.shape[1]
     everyone = fellows * particles
@@ -357,15 +390,17 @@
             jax.ShapeDtypeStruct((everyone, LANES, LANES), BF16),
             jax.ShapeDtypeStruct((fellows, particles, LANES), jnp.int32),
         ),
-        in_specs=vmem_specs(3),
+        in_specs=[smem] + vmem_specs(4),
         out_specs=tuple(vmem_specs(3)),
         scratch_shapes=[
             VMEM((fellows, packs, angles, LANES), BF16),
             VMEM((owners,) + mine.shape, BF16),
             pltpu.SMEM((fellows, particles, LANES), jnp.int32),
-            VMEM((owners * slots, tall_rows, LANES), BF16),
+            VMEM((owners * per_owner, tall_rows, LANES), BF16),
             VMEM((particles * top, LANES), F32),
             VMEM((particles * top, LANES), F32),
+            VMEM((per_pack, LANES, LANES), BF16),
+            VMEM((per_den, LANES, LANES), BF16),
             dma((2,)),
             dma((fellows,)),
             dma((fellows,)),
@@ -377,24 +412,24 @@
             dma((fellows, fellows)),
         ],
         compiler_params=pltpu.CompilerParams(collective_id=0, has_side_effects=True),
-    )(send, mine, rows)
+    )(class_place, send, mine, rows, sigma2.reshape(1, shells))
     row_list = tall[:, :, :top].reshape(everyone, top)
     sums = pl.pallas_call(
         functools.partial(total_kernel, dims),
         out_shape=jax.ShapeDtypeStruct(
-            (owners, slots // per_pack + slots // per_den, angles, LANES), BF16
+            (owners, slots // per_pack - (-slots // per_den), angles, LANES), BF16
         ),
-        in_specs=[smem] + vmem_specs(2),
+        in_specs=[smem, smem] + vmem_specs(2),
         out_specs=pl.BlockSpec(memory_space=pltpu.VMEM),
         scratch_shapes=[
-            VMEM((owners * slots, angles, LANES), F32),
+            VMEM((owners * per_owner, angles, LANES), F32),
             VMEM((pairs, 2 * top, LANES), F32),
             VMEM((pairs, 2 * top, LANES), F32),
         ],
-    )(row_list, parts, weights)
+    )(class_place, row_list, parts, weights)
     share = pl.pallas_call(
-        functools.partial(gather_kernel, "cls", owners),
-        out_shape=jax.ShapeDtypeStruct(sums.shape[1:], F32),
+        functools.partial(gather_kernel, "cls", owners, half, slots),
+        out_shape=jax.ShapeDtypeStruct((slots // per_pack, LANES, angles), F32),
         in_specs=vmem_specs(1),
         out_specs=pl.BlockSpec(memory_space=pltpu.VMEM),
         scratch_shapes=[
@@ -404,12 +439,7 @@
         ],
         compiler_params=pltpu.CompilerParams(collective_id=2, has_side_effects=True),
     )(sums)
-    num_packs = slots // per_pack
-    num = share[:num_packs].reshape(num_packs, angles, per_pack, 2, half)
-    num = num.transpose(0, 2, 4, 3, 1).reshape(slots, half, 2, angles)[:per_owner]
-    den = share[num_packs:].reshape(-1, angles, per_den, half)
-    den = den.transpose(0, 2, 3, 1).reshape(slots, half, 1, angles)[:per_owner]
-    return (num / (den + 1.0)).reshape(per_owner, -1)
+    return share.reshape(slots * width, angles)[: per_owner * width].reshape(per_owner, -1)
 
 
 def solution(mesh):

time: 62 us -> 58.9 us (0.950)
  other arithmetic: 2.88 us -> 0.82 us
  local copies, waits for them, and re-layouts: 8.92 us -> 8.04 us
    slice x4 -> x1, local copies, waits for them, and re-layouts: 1.84 us -> 0.91 us  [on_device(): share.reshape(slots * width, angles)[:per_owner * width]]
    reduce_sum x1 -> x0, other arithmetic: 0.91 us -> none  [on_device(): jnp.sum(jnp.where(lookup, class_place[None, None, :], 0), axis=2)]
    unnamed x6 -> x3, local copies, waits for them, and re-layouts: 0.01 us -> 0.8 us
    div x2 -> x0, other arithmetic: 0.74 us -> none  [the longest x1 0.72 us: on_device(): 1.0 / sigma2]
where the time goes in v2:
time: 58.9 us; the launch traced here: 58.6 us
  Pallas kernels  49.7 us (84%)
  local copies, waits for them, and re-layouts  8.04 us (14%)
  other arithmetic  0.82 us (1%)
    pallas_call x1, Pallas kernels, on_device(): pl.pallas_call(functools.partial(score_kernel, dims), out_shape=(jax.Shap...  26.6 us
    pallas_call x1, Pallas kernels, on_device(): pl.pallas_call(functools.partial(gather_kernel, 'cls', owners, half, slot...  13.6 us
    pallas_call x1, Pallas kernels, on_device(): pl.pallas_call(functools.partial(total_kernel, dims), out_shape=jax.Shape...  9.39 us
    reshape x2, local copies, waits for them, and re-layouts, on_device(): images.reshape(particles // per_pack, per_pack, fellows, width, angles)  2.16 us
    reshape x2, local copies, waits for them, and re-layouts, on_device(): den = ctf.reshape(particles // per_den, per_den, fellows, half, angles)  1.46 us

profile of v2, /device:TPU:0, one launch (start us, length us, event | category | flops | bytes accessed | tf_op | source)
XLA Modules:
  0.0 58.6 jit_solution(12613579820624979240)
XLA Ops:
  0.0 0.0 copy-start
  0.0 0.8 %copy.15 = s32[16,4]{1,0:T(8,128)S(1)} copy(s32[16,4]{0,1:T(4,128)} %param.8) | data formatting | bytes 512 | tf_op args[2]
  0.8 0.6 %pad.9.t_ref = s32[16,128]{1,0:T(8,128)} pad(s32[16,4]{1,0:T(8,128)S(1)} %copy.15, s32[]{:T(128)} %constant.2.clone.1), padding=0_0x0_124 | pad | bytes 8452 | tf_op jit(solution)/shard_map/jit(_pad)/pad | solution.py:378
  1.4 0.0 copy-done
  1.4 0.2 reshape.34
  1.6 0.1 rev.3
  1.7 0.7 %copy.16.r_ref = bf16[2,72,128]{2,1,0:T(8,128)(2,1)} copy(bf16[2,72,128]{1,2,0:T(8,128)(2,1)S(1)} %bitcast.16) | data formatting | bytes 73728 | tf_op jit(solution)/shard_map/reshape | solution.py:377
  2.4 1.4 %reshape.32 = bf16[2,8,4,16,72]{4,3,2,1,0:T(8,128)(2,1)S(1)} reshape(bf16[16,4608]{1,0:T(8,128)(2,1)} %param.7) | data formatting | bytes 294912 | tf_op jit(solution)/shard_map/reshape | solution.py:371
  3.9 0.1 copy.14
  4.0 2.1 %reshape.30 = bf16[4,4,4,32,72]{4,3,2,1,0:T(8,128)(2,1)S(1)} reshape(bf16[16,9216]{1,0:T(8,128)(2,1)} %param.6) | data formatting | bytes 589824 | tf_op jit(solution)/shard_map/reshape | solution.py:369
  6.2 0.2 copy.13
  6.4 0.8 %pad_maximum_fusion.w_ref = bf16[4,6,72,128]{3,2,1,0:T(8,128)(2,1)} fusion(bf16[4,2,72,128]{3,2,1,0:T(8,128)(2,1)S(1)} %copy.14, bf16[4,4,72,128]{3,2,1,0:T(8,128)(2,1)S(1)} %copy.13), kind=kLoop, calls=%fused_computation | loop fusion | flops 221184 | bytes 884736 | tf_op jit(solution)/shard_map/concatenate | solution.py:373
  7.3 26.6 %shard_map.64 = (f32[4,256,128]{2,1,0:T(8,128)}, bf16[64,128,128]{2,1,0:T(8,128)(2,1)}, s32[4,16,128]{2,1,0:T(8,128)}) custom-call(s32[56]{0:T(128)} %place_ref.3, bf16[4,6,72,128]{3,2,1,0:T(8,128)(2,1)} %pad_maximum_fusion.w_ref, bf16[2,72,128]{2,1,0:T(8,128)(2,1)} %copy.16.r_ref, s32[16,128]{1,0:T(8,128)} %pad.9.t_ref, f32[1,64]{1,0:T(1,128)} %bitcast.18), custom_call_target="tpu_custom_call" | custom-call | tf_op jit(solution)/shard_map/pallas_call | solution.py:386
  33.9 9.4 %shard_map.65.x_ref = bf16[8,3,72,128]{3,2,1,0:T(8,128)(2,1)} custom-call(s32[56]{0:T(128)} %place_ref.3, s32[64,4]{1,0:T(8,128)} %bitcast.17, f32[4,256,128]{2,1,0:T(8,128)} %get-tuple-element.9.parts, bf16[64,128,128]{2,1,0:T(8,128)(2,1)} %get-tuple-element.10.weights_ref), custom_call_target="tpu_custom_call" | custom-call | tf_op jit(solution)/shard_map/pallas_call | solution.py:417
  43.3 13.6 %shard_map.66 = f32[2,128,72]{2,1,0:T(8,128)} custom-call(bf16[8,3,72,128]{3,2,1,0:T(8,128)(2,1)} %shard_map.65.x_ref), custom_call_target="tpu_custom_call" | custom-call | tf_op jit(solution)/shard_map/pallas_call | solution.py:430
  56.9 0.9 %slice.8 = f32[224,72]{1,0:T(8,128)S(1)} slice(f32[256,72]{1,0:T(8,128)} %bitcast.15), slice={[0:224], [0:72]} | slice | bytes 129024 | tf_op jit(solution)/shard_map/slice | solution.py:442
  57.9 0.8 %reshape.39 = f32[7,2304]{1,0:T(8,128)} reshape(f32[224,72]{1,0:T(8,128)S(1)} %slice.8) | data formatting | bytes 129024 | tf_op jit(solution)/shard_map/reshape | solution.py:442
  (4 shorter events, 0.1 us)
Async XLA Ops:
  0.0 1.4 %copy-start = (bf16[7,9216]{1,0:T(8,128)(2,1)S(1)}, bf16[7,9216]{1,0:T(8,128)(2,1)}, u32[]{:S(2)}) copy-start(bf16[7,9216]{1,0:T(8,128)(2,1)} %param.10) | copy-start | bytes 387076

commit v3 on v2

--- a/solution.py
+++ b/solution.py
@@ -39,16 +39,16 @@
 
 
 def score_kernel(
-    dims, place_ref, w_ref, r_ref, t_ref, sigma_ref, parts, weights_ref, tall, wall, rall, rows_ref,
+    dims, place_ref, n_ref, d_ref, r_ref, t_ref, sigma_ref, parts, weights_ref, tall, nall, dall,
+    rall, rows_ref,
     table, low, high, pick_num, pick_den,
-    own_sem, ws, wr, rs, rr, ts, tr, ls, lr,
+    own_sem, ns, nr, ds, dr, rs, rr, fs, fr, ts, tr, ls, lr,
 ):
     fellows, particles, owners, per_owner, slots, top, angles, half = dims
     width = 2 * half
     per_pack = LANES // width
     per_den = LANES // half
     tall_rows = table.shape[1]
-    num_packs = particles // per_pack
     tiles = angles // 8
     cut = (tiles // 2 + tiles % 2) * 8
     my_owner = lax.axis_index("cls")
@@ -72,13 +72,22 @@
         peer = lax.rem(my_fellow + step, fellows)
         row_copies.append(remote(t_ref, tall.at[my_fellow], ts.at[step], tr.at[step], "img", peer))
         image_copies.append(
-            remote(w_ref.at[peer], wall.at[my_fellow], ws.at[step], wr.at[step], "img", peer)
+            (
+                remote(n_ref.at[peer], nall.at[my_fellow], ns.at[step], nr.at[step], "img", peer),
+                remote(d_ref.at[peer], dall.at[my_fellow], ds.at[step], dr.at[step], "img", peer),
+            )
         )
-    for step in range(1, owners):
-        peer = lax.rem(my_owner + step, owners)
+    partner = my_owner + 1 - 2 * lax.rem(my_owner, 2)
+    strides = owners // 2
+    for step in range(1, strides):
+        peer = lax.rem(my_owner + 2 * step, owners)
         ref_copies.append(remote(r_ref, rall.at[my_owner], rs.at[step], rr.at[step], "cls", peer))
-    for copy in row_copies + ref_copies + image_copies:
+    forwards = [remote(r_ref, rall.at[my_owner], fs.at[0], fr.at[0], "cls", partner)]
+    for copy in ref_copies[::-1] + forwards + row_copies:
         copy.start()
+    for num_copy, den_copy in image_copies:
+        num_copy.start()
+        den_copy.start()
     own_rows = pltpu.make_async_copy(t_ref, tall.at[my_fellow], own_sem.at[0])
     own_rows.start()
 
@@ -102,15 +111,15 @@
         inverse = jnp.where(row_lane // half == part, pltpu.roll(spread, shift, 1), inverse)
     inverse = inverse[0:1]
 
-    def place(fellow, read):
+    def place(fellow, read_num, read_den):
         def some(u, carry):
             for g in range(per_den):
                 num = jnp.dot(
-                    read(u * (per_den // per_pack) + g // per_pack),
+                    read_num(u * (per_den // per_pack) + g // per_pack),
                     pick_num[g % per_pack],
                     preferred_element_type=F32,
                 )
-                den = jnp.dot(read(num_packs + u), pick_den[g], preferred_element_type=F32)
+                den = jnp.dot(read_den(u), pick_den[g], preferred_element_type=F32)
                 joined = jnp.where(lane < width, num, den) * (den * inverse)
                 weights_ref[fellow * particles + u * per_den + g] = jnp.concatenate(
                     [joined, zero_tail], axis=0
@@ -130,22 +139,30 @@
                 [joined, jnp.zeros((tall_rows - angles, LANES), F32)], axis=0
             ).astype(BF16)
 
-    place(my_fellow, lambda u: w_ref[my_fellow, u])
     tabulate(my_owner, lambda u: r_ref[u])
+    for step in range(1, strides):
+        holder = lax.rem(my_owner + owners - 2 * step, owners)
+        ref_copies[step - 1].wait_recv()
+        forward = remote(rall.at[holder], rall.at[holder], fs.at[step], fr.at[step], "cls", partner)
+        forward.start()
+        forwards.append(forward)
+        tabulate(holder, lambda u: rall[holder, u])
     own_rows.wait()
     for copy in row_copies:
         copy.wait_recv()
     to_smem = pltpu.make_async_copy(tall, rows_ref, own_sem.at[1])
     to_smem.start()
-    for step in range(1, max(owners, fellows)):
-        if step < fellows:
-            image_copies[step - 1].wait_recv()
+    place(my_fellow, lambda u: n_ref[my_fellow, u], lambda u: d_ref[my_fellow, u])
+    for step in range(max(strides, fellows)):
+        if step < strides:
+            forwards[step].wait_recv()
+            holder = lax.rem(partner + owners - 2 * step, owners)
+            tabulate(holder, lambda u: rall[holder, u])
+        if 0 < step < fellows:
+            for copy in image_copies[step - 1]:
+                copy.wait_recv()
             source = lax.rem(my_fellow + fellows - step, fellows)
-            place(source, lambda u: wall[source, u])
-        if step < owners:
-            ref_copies[step - 1].wait_recv()
-            holder = lax.rem(my_owner + owners - step, owners)
-            tabulate(holder, lambda u: rall[holder, u])
+            place(source, lambda u: nall[source, u], lambda u: dall[source, u])
     to_smem.wait()
 
     batch = 8
@@ -155,7 +172,7 @@
         highs = []
         for k in range(batch):
             i = begin + k
-            refs = jnp.concatenate([table[place_ref[rows_ref[fellow, i, j]]] for j in range(top)], axis=0)
+            refs = jnp.concatenate([table[place_ref[rows_ref[fellow, j, i]]] for j in range(top)], axis=0)
             grid = lax.dot_general(
                 refs,
                 weights_ref[fellow * particles + i],
@@ -201,8 +218,11 @@
             copy = remote(place_at, place_at, ls.at[step, fellow], lr.at[step, fellow], "img", peer)
             copy.start()
             part_copies.append(copy)
-    for copy in row_copies + ref_copies + image_copies:
+    for copy in row_copies + ref_copies + forwards:
         copy.wait_send()
+    for num_copy, den_copy in image_copies:
+        num_copy.wait_send()
+        den_copy.wait_send()
     for copy in part_copies:
         copy.wait()
 
@@ -270,7 +290,9 @@
                     turned.append(second)
             circle = jnp.concatenate(turned, axis=0).astype(BF16)
             grid = jnp.dot(circle, weights_ref[i], preferred_element_type=F32)
-            spots = [place_ref[rows_ref[i, j]] for j in range(top)]
+            spots = [
+                place_ref[rows_ref[i // particles, j, i % particles]] for j in range(top)
+            ]
             held = [acc[spot] for spot in spots]
             for j in range(top):
                 acc[spots[j]] = held[j] + grid[j * tall_rows : j * tall_rows + angles]
@@ -370,14 +392,12 @@
     num = num.transpose(2, 0, 4, 1, 3).reshape(fellows, -1, angles, LANES)
     den = ctf.reshape(particles // per_den, per_den, fellows, half, angles)
     den = den.transpose(2, 0, 4, 1, 3).reshape(fellows, -1, angles, LANES)
-    send = jnp.concatenate([num, den], axis=1)
     mine = lax.dynamic_slice_in_dim(references, my_fellow * (width * angles), width * angles, 1)
     mine = jnp.pad(mine, ((0, slots - per_owner), (0, 0)))
     mine = mine.reshape(slots // per_pack, per_pack, width, angles)[..., ::-1]
     mine = mine.transpose(0, 3, 1, 2).reshape(-1, angles, LANES)
-    rows = jnp.pad(classes, ((0, 0), (0, LANES - top)))
-
-    packs = send.shape[1]
+    rows = classes.T
+
     everyone = fellows * particles
     tall_rows = -(-angles // 16) * 16
     pairs = everyone // 2
@@ -388,14 +408,15 @@
         out_shape=(
             jax.ShapeDtypeStruct((fellows, everyone * top, LANES), F32),
             jax.ShapeDtypeStruct((everyone, LANES, LANES), BF16),
-            jax.ShapeDtypeStruct((fellows, particles, LANES), jnp.int32),
+            jax.ShapeDtypeStruct((fellows, top, particles), jnp.int32),
         ),
-        in_specs=[smem] + vmem_specs(4),
+        in_specs=[smem] + vmem_specs(5),
         out_specs=tuple(vmem_specs(3)),
         scratch_shapes=[
-            VMEM((fellows, packs, angles, LANES), BF16),
+            VMEM(num.shape, BF16),
+            VMEM(den.shape, BF16),
             VMEM((owners,) + mine.shape, BF16),
-            pltpu.SMEM((fellows, particles, LANES), jnp.int32),
+            pltpu.SMEM((fellows, top, particles), jnp.int32),
             VMEM((owners * per_owner, tall_rows, LANES), BF16),
             VMEM((particles * top, LANES), F32),
             VMEM((particles * top, LANES), F32),
@@ -404,6 +425,10 @@
             dma((2,)),
             dma((fellows,)),
             dma((fellows,)),
+            dma((fellows,)),
+            dma((fellows,)),
+            dma((owners,)),
+            dma((owners,)),
             dma((owners,)),
             dma((owners,)),
             dma((fellows,)),
@@ -412,8 +437,7 @@
             dma((fellows, fellows)),
         ],
         compiler_params=pltpu.CompilerParams(collective_id=0, has_side_effects=True),
-    )(class_place, send, mine, rows, sigma2.reshape(1, shells))
-    row_list = tall[:, :, :top].reshape(everyone, top)
+    )(class_place, num, den, mine, rows, sigma2.reshape(1, shells))
     sums = pl.pallas_call(
         functools.partial(total_kernel, dims),
         out_shape=jax.ShapeDtypeStruct(
@@ -426,7 +450,7 @@
             VMEM((pairs, 2 * top, LANES), F32),
             VMEM((pairs, 2 * top, LANES), F32),
         ],
-    )(class_place, row_list, parts, weights)
+    )(class_place, tall, parts, weights)
     share = pl.pallas_call(
         functools.partial(gather_kernel, "cls", owners, half, slots),
         out_shape=jax.ShapeDtypeStruct((slots // per_pack, LANES, angles), F32),

time: 58.9 us -> 59.9 us (1.017)
  Pallas kernels: 49.7 us -> 50.6 us
  local copies, waits for them, and re-layouts: 8.04 us -> 8.88 us
  other arithmetic: 0.82 us -> 0 us
    pallas_call x1, Pallas kernels: 26.6 us -> 27.7 us  [on_device(): pl.pallas_call(functools.partial(score_kernel, dims), out_shape=(jax.Shap...]
    concatenate x1 -> x0, other arithmetic: 0.82 us -> none  [on_device(): send = jnp.concatenate([num, den], axis=1)]
    reshape x1, local copies, waits for them, and re-layouts: 0.23 us -> 0.91 us  [on_device(): num = num.transpose(2, 0, 4, 1, 3).reshape(fellows, -1, angles, LANES)]
    reshape x1, local copies, waits for them, and re-layouts: 0.14 us -> 0.79 us  [on_device(): den = den.transpose(2, 0, 4, 1, 3).reshape(fellows, -1, angles, LANES)]
    pad x1 -> x0, local copies, waits for them, and re-layouts: 0.6 us -> none  [on_device(): rows = jnp.pad(classes, ((0, 0), (0, LANES - top)))]
where the time goes in v3:
time: 59.9 us; the launch traced here: 59.6 us
  Pallas kernels  50.6 us (84%)
  local copies, waits for them, and re-layouts  8.88 us (15%)
    pallas_call x1, Pallas kernels, on_device(): pl.pallas_call(functools.partial(score_kernel, dims), out_shape=(jax.Shap...  27.7 us
    pallas_call x1, Pallas kernels, on_device(): pl.pallas_call(functools.partial(gather_kernel, 'cls', owners, half, slot...  13.6 us
    pallas_call x1, Pallas kernels, on_device(): pl.pallas_call(functools.partial(total_kernel, dims), out_shape=jax.Shape...  9.35 us
    reshape x2, local copies, waits for them, and re-layouts, on_device(): images.reshape(particles // per_pack, per_pack, fellows, width, angles)  2.16 us
    reshape x2, local copies, waits for them, and re-layouts, on_device(): den = ctf.reshape(particles // per_den, per_den, fellows, half, angles)  1.46 us

profile of v3, /device:TPU:0, one launch (start us, length us, event | category | flops | bytes accessed | tf_op | source)
XLA Modules:
  0.0 59.6 jit_solution(4196792019149682604)
XLA Ops:
  0.0 0.0 copy-start
  0.0 0.9 %copy-done = bf16[7,9216]{1,0:T(8,128)(2,1)S(1)} copy-done((bf16[7,9216]{1,0:T(8,128)(2,1)S(1)}, bf16[7,9216]{1,0:T(8,128)(2,1)}, u32[]{:S(2)}) %copy-start) | copy-done | bytes 129048
  0.9 0.2 reshape.31
  1.1 0.1 rev.3
  1.2 0.7 %copy.14.r_ref = bf16[2,72,128]{2,1,0:T(8,128)(2,1)} copy(bf16[2,72,128]{1,2,0:T(8,128)(2,1)S(1)} %bitcast.15) | data formatting | bytes 73728 | tf_op jit(solution)/shard_map/reshape | solution.py:398
  1.9 1.4 %reshape.29 = bf16[2,8,4,16,72]{4,3,2,1,0:T(8,128)(2,1)S(1)} reshape(bf16[16,4608]{1,0:T(8,128)(2,1)} %param.7) | data formatting | bytes 294912 | tf_op jit(solution)/shard_map/reshape | solution.py:393
  3.4 0.8 %copy.13.d_ref = bf16[4,2,72,128]{3,2,1,0:T(8,128)(2,1)} copy(bf16[4,2,72,128]{2,3,1,0:T(8,128)(2,1)S(1)} %bitcast.13) | data formatting | bytes 294912 | tf_op jit(solution)/shard_map/reshape | solution.py:394
  4.2 2.1 %reshape.27 = bf16[4,4,4,32,72]{4,3,2,1,0:T(8,128)(2,1)S(1)} reshape(bf16[16,9216]{1,0:T(8,128)(2,1)} %param.6) | data formatting | bytes 589824 | tf_op jit(solution)/shard_map/reshape | solution.py:391
  6.3 0.9 %copy.12.n_ref = bf16[4,4,72,128]{3,2,1,0:T(8,128)(2,1)} copy(bf16[4,4,72,128]{2,3,1,0:T(8,128)(2,1)S(1)} %bitcast.12) | data formatting | bytes 589824 | tf_op jit(solution)/shard_map/reshape | solution.py:392
  7.3 27.7 %shard_map.64 = (f32[4,256,128]{2,1,0:T(8,128)}, bf16[64,128,128]{2,1,0:T(8,128)(2,1)}, s32[4,4,16]{2,1,0:T(4,128)}) custom-call(s32[56]{0:T(128)} %place_ref.3, bf16[4,4,72,128]{3,2,1,0:T(8,128)(2,1)} %copy.12.n_ref, bf16[4,2,72,128]{3,2,1,0:T(8,128)(2,1)} %copy.13.d_ref, bf16[2,72,128]{2,1,0:T(8,128)(2,1)} %copy.14.r_ref, s32[4,16]{1,0:T(4,128)} %bitcast.16, ...), custom_call_target="tpu_custom_call" | custom-call | tf_op jit(solution)/shard_map/pallas_call | solution.py:406
  35.0 9.4 %shard_map.65.x_ref = bf16[8,3,72,128]{3,2,1,0:T(8,128)(2,1)} custom-call(s32[56]{0:T(128)} %place_ref.3, s32[4,4,16]{2,1,0:T(4,128)} %get-tuple-element.8.rows_ref, f32[4,256,128]{2,1,0:T(8,128)} %get-tuple-element.9.parts, bf16[64,128,128]{2,1,0:T(8,128)(2,1)} %get-tuple-element.10.weights_ref), custom_call_target="tpu_custom_call" | custom-call | tf_op jit(solution)/shard_map/pallas_call | solution.py:441
  44.3 13.6 %shard_map.66 = f32[2,128,72]{2,1,0:T(8,128)} custom-call(bf16[8,3,72,128]{3,2,1,0:T(8,128)(2,1)} %shard_map.65.x_ref), custom_call_target="tpu_custom_call" | custom-call | tf_op jit(solution)/shard_map/pallas_call | solution.py:454
  57.9 0.9 %slice.4 = f32[224,72]{1,0:T(8,128)S(1)} slice(f32[256,72]{1,0:T(8,128)} %bitcast.14), slice={[0:224], [0:72]} | slice | bytes 129024 | tf_op jit(solution)/shard_map/slice | solution.py:466
  58.8 0.8 %reshape.35 = f32[7,2304]{1,0:T(8,128)} reshape(f32[224,72]{1,0:T(8,128)S(1)} %slice.4) | data formatting | bytes 129024 | tf_op jit(solution)/shard_map/reshape | solution.py:466
  (4 shorter events, 0.1 us)
Async XLA Ops:
  0.0 0.9 %copy-start = (bf16[7,9216]{1,0:T(8,128)(2,1)S(1)}, bf16[7,9216]{1,0:T(8,128)(2,1)}, u32[]{:S(2)}) copy-start(bf16[7,9216]{1,0:T(8,128)(2,1)} %param.10) | copy-start | bytes 387076

commit v4 on v2

--- a/solution.py
+++ b/solution.py
@@ -130,22 +130,17 @@
                 [joined, jnp.zeros((tall_rows - angles, LANES), F32)], axis=0
             ).astype(BF16)
 
+    tabulate(my_owner, lambda u: r_ref[u])
     place(my_fellow, lambda u: w_ref[my_fellow, u])
-    tabulate(my_owner, lambda u: r_ref[u])
     own_rows.wait()
     for copy in row_copies:
         copy.wait_recv()
     to_smem = pltpu.make_async_copy(tall, rows_ref, own_sem.at[1])
     to_smem.start()
-    for step in range(1, max(owners, fellows)):
-        if step < fellows:
-            image_copies[step - 1].wait_recv()
-            source = lax.rem(my_fellow + fellows - step, fellows)
-            place(source, lambda u: wall[source, u])
-        if step < owners:
-            ref_copies[step - 1].wait_recv()
-            holder = lax.rem(my_owner + owners - step, owners)
-            tabulate(holder, lambda u: rall[holder, u])
+    for step in range(1, owners):
+        ref_copies[step - 1].wait_recv()
+        holder = lax.rem(my_owner + owners - step, owners)
+        tabulate(holder, lambda u: rall[holder, u])
     to_smem.wait()
 
     batch = 8
@@ -181,7 +176,11 @@
 
     part_copies = []
     chunk = particles * top
-    for fellow in range(fellows):
+    for turn in range(fellows):
+        fellow = lax.rem(my_fellow + fellows - turn, fellows)
+        if turn:
+            image_copies[turn - 1].wait_recv()
+            place(fellow, lambda u: wall[fellow, u])
 
         def some(b, carry):
             score(fellow, b * batch)
@@ -194,11 +193,12 @@
         total = roll(lo, 1) + jnp.where(spot < cut, roll(lo, 1 - angles), 0.0)
         back = angles - 1 - cut
         total = total + roll(hi, -back) + jnp.where(spot >= cut + 1, roll(hi, cut + 1), 0.0)
-        place_at = parts.at[my_fellow, pl.ds(fellow * chunk, chunk)]
-        parts[my_fellow, pl.ds(fellow * chunk, chunk)] = jnp.where(spot < angles, total, 0.0)
+        begin = pl.multiple_of(fellow * chunk, chunk)
+        place_at = parts.at[my_fellow, pl.ds(begin, chunk)]
+        parts[my_fellow, pl.ds(begin, chunk)] = jnp.where(spot < angles, total, 0.0)
         for step in range(1, fellows):
             peer = lax.rem(my_fellow + step, fellows)
-            copy = remote(place_at, place_at, ls.at[step, fellow], lr.at[step, fellow], "img", peer)
+            copy = remote(place_at, place_at, ls.at[step, turn], lr.at[step, turn], "img", peer)
             copy.start()
             part_copies.append(copy)
     for copy in row_copies + ref_copies + image_copies:

time: 58.9 us -> 60.9 us (1.034); the launches traced: 58.6 us -> 59.8 us
  Pallas kernels: 49.7 us -> 50.9 us
    pallas_call x1, Pallas kernels: 26.6 us -> 27.4 us  [on_device(): pl.pallas_call(functools.partial(score_kernel, dims), out_shape=(jax.Shap...]
where the time goes in v4:
time: 60.9 us; the launch traced here: 59.8 us
  Pallas kernels  50.9 us (84%)
  local copies, waits for them, and re-layouts  8.04 us (13%)
  other arithmetic  0.82 us (1%)
    pallas_call x1, Pallas kernels, on_device(): pl.pallas_call(functools.partial(score_kernel, dims), out_shape=(jax.Shap...  27.4 us
    pallas_call x1, Pallas kernels, on_device(): pl.pallas_call(functools.partial(gather_kernel, 'cls', owners, half, slot...  14.1 us
    pallas_call x1, Pallas kernels, on_device(): pl.pallas_call(functools.partial(total_kernel, dims), out_shape=jax.Shape...  9.38 us
    reshape x2, local copies, waits for them, and re-layouts, on_device(): images.reshape(particles // per_pack, per_pack, fellows, width, angles)  2.16 us
    reshape x2, local copies, waits for them, and re-layouts, on_device(): den = ctf.reshape(particles // per_den, per_den, fellows, half, angles)  1.46 us

profile of v4, /device:TPU:0, one launch (start us, length us, event | category | flops | bytes accessed | tf_op | source)
XLA Modules:
  0.0 59.8 jit_solution(9740889158650202726)
XLA Ops:
  0.0 0.0 copy-start
  0.0 0.8 %copy.15 = s32[16,4]{1,0:T(8,128)S(1)} copy(s32[16,4]{0,1:T(4,128)} %param.8) | data formatting | bytes 512 | tf_op args[2]
  0.8 0.6 %pad.9.t_ref = s32[16,128]{1,0:T(8,128)} pad(s32[16,4]{1,0:T(8,128)S(1)} %copy.15, s32[]{:T(128)} %constant.2.clone.1), padding=0_0x0_124 | pad | bytes 8452 | tf_op jit(solution)/shard_map/jit(_pad)/pad | solution.py:378
  1.4 0.0 copy-done
  1.4 0.2 reshape.34
  1.6 0.1 rev.3
  1.7 0.7 %copy.16.r_ref = bf16[2,72,128]{2,1,0:T(8,128)(2,1)} copy(bf16[2,72,128]{1,2,0:T(8,128)(2,1)S(1)} %bitcast.16) | data formatting | bytes 73728 | tf_op jit(solution)/shard_map/reshape | solution.py:377
  2.4 1.4 %reshape.32 = bf16[2,8,4,16,72]{4,3,2,1,0:T(8,128)(2,1)S(1)} reshape(bf16[16,4608]{1,0:T(8,128)(2,1)} %param.7) | data formatting | bytes 294912 | tf_op jit(solution)/shard_map/reshape | solution.py:371
  3.9 0.1 copy.14
  4.0 2.1 %reshape.30 = bf16[4,4,4,32,72]{4,3,2,1,0:T(8,128)(2,1)S(1)} reshape(bf16[16,9216]{1,0:T(8,128)(2,1)} %param.6) | data formatting | bytes 589824 | tf_op jit(solution)/shard_map/reshape | solution.py:369
  6.2 0.2 copy.13
  6.4 0.8 %pad_maximum_fusion.w_ref = bf16[4,6,72,128]{3,2,1,0:T(8,128)(2,1)} fusion(bf16[4,2,72,128]{3,2,1,0:T(8,128)(2,1)S(1)} %copy.14, bf16[4,4,72,128]{3,2,1,0:T(8,128)(2,1)S(1)} %copy.13), kind=kLoop, calls=%fused_computation | loop fusion | flops 221184 | bytes 884736 | tf_op jit(solution)/shard_map/concatenate | solution.py:373
  7.3 27.4 %shard_map.64 = (f32[4,256,128]{2,1,0:T(8,128)}, bf16[64,128,128]{2,1,0:T(8,128)(2,1)}, s32[4,16,128]{2,1,0:T(8,128)}) custom-call(s32[56]{0:T(128)} %place_ref.3, bf16[4,6,72,128]{3,2,1,0:T(8,128)(2,1)} %pad_maximum_fusion.w_ref, bf16[2,72,128]{2,1,0:T(8,128)(2,1)} %copy.16.r_ref, s32[16,128]{1,0:T(8,128)} %pad.9.t_ref, f32[1,64]{1,0:T(1,128)} %bitcast.18), custom_call_target="tpu_custom_call" | custom-call | tf_op jit(solution)/shard_map/pallas_call | solution.py:386
  34.7 9.4 %shard_map.65.x_ref = bf16[8,3,72,128]{3,2,1,0:T(8,128)(2,1)} custom-call(s32[56]{0:T(128)} %place_ref.3, s32[64,4]{1,0:T(8,128)} %bitcast.17, f32[4,256,128]{2,1,0:T(8,128)} %get-tuple-element.9.parts, bf16[64,128,128]{2,1,0:T(8,128)(2,1)} %get-tuple-element.10.weights_ref), custom_call_target="tpu_custom_call" | custom-call | tf_op jit(solution)/shard_map/pallas_call | solution.py:417
  44.0 14.1 %shard_map.66 = f32[2,128,72]{2,1,0:T(8,128)} custom-call(bf16[8,3,72,128]{3,2,1,0:T(8,128)(2,1)} %shard_map.65.x_ref), custom_call_target="tpu_custom_call" | custom-call | tf_op jit(solution)/shard_map/pallas_call | solution.py:430
  58.2 0.9 %slice.8 = f32[224,72]{1,0:T(8,128)S(1)} slice(f32[256,72]{1,0:T(8,128)} %bitcast.15), slice={[0:224], [0:72]} | slice | bytes 129024 | tf_op jit(solution)/shard_map/slice | solution.py:442
  59.1 0.8 %reshape.39 = f32[7,2304]{1,0:T(8,128)} reshape(f32[224,72]{1,0:T(8,128)S(1)} %slice.8) | data formatting | bytes 129024 | tf_op jit(solution)/shard_map/reshape | solution.py:442
  (4 shorter events, 0.1 us)
Async XLA Ops:
  0.0 1.4 %copy-start = (bf16[7,9216]{1,0:T(8,128)(2,1)S(1)}, bf16[7,9216]{1,0:T(8,128)(2,1)}, u32[]{:S(2)}) copy-start(bf16[7,9216]{1,0:T(8,128)(2,1)} %param.10) | copy-start | bytes 387076
